TPU v7x, 32 devices: a whole 2x2x4 slice. The times are simulated.
32 devices in a mesh: grp: 4 (over z), col: 8 (over y, x, core).
Axes of the slice: x: 2, y: 2, z: 4, core: 2. Of those that a mesh axis runs over, the one named last changes fastest.
Arguments:
- inverse: bfloat16 [4, 8192, 8192], P('grp', None, 'col'), as said below
- right_side: float32 [4, 8192, 256], P('grp', 'col'), may hold values from -6 to 6
- penalty: float32 [256], replicated, may hold values from 0.2 to 6
Outputs:
- consensus: float32 [8192, 256], P('col')
- duals: float32 [4, 8192, 256], P('grp', 'col')
Inputs may be any that keep to these rules, and one draw needn't show every extreme that they name: Each inverse[g] is symmetric.
All inputs are finite; a program needn't handle non-finite values.
Results may differ from a plain program's by a relative error of at most 0.0042.
Values may be sent and summed in bfloat16 or wider, within the bound.
A program may use at most 64 MiB of HBM per device.

v0:
```python
import jax
import jax.numpy as jnp
from jax import lax
from jax.sharding import PartitionSpec as P

ITERS = 3


def soft_shrink(values, limit):
    return jnp.sign(values) * jnp.maximum(jnp.abs(values) - limit, 0.0)


def apply_inverse(columns, shifted):
    return lax.dot_general(
        columns,
        lax.all_gather(shifted, "col", axis=0, tiled=True),
        (((0,), (0,)), ((), ())),
        preferred_element_type=jnp.float32,
    )


def agree(summed_in, limit, groups):
    summed = lax.psum(summed_in, "grp")
    return soft_shrink(summed / groups, limit[None, :])


def update_paths(columns, right_part, consensus, duals, limit, groups):
    shifted = (right_part + consensus - duals).astype(jnp.bfloat16)
    primal = apply_inverse(columns, shifted)
    consensus = agree(primal + duals, limit, groups)
    duals = duals + primal - consensus
    return (consensus, duals)


def on_device(inverse, right_side, penalty):
    columns = inverse[0]
    right_part = right_side[0]
    groups = lax.axis_size("grp")
    limit = penalty / groups
    consensus = jnp.zeros(right_part.shape, jnp.float32)
    duals = jnp.zeros(right_part.shape, jnp.float32)
    for step in range(ITERS):
        consensus, duals = update_paths(columns, right_part, consensus, duals, limit, groups)
    return (consensus, duals[None])


def solution(mesh):
    in_specs = (P("grp", None, "col"), P("grp", "col", None), P())
    out_specs = (P("col", None), P("grp", "col", None))
    return jax.shard_map(
        on_device, mesh=mesh, in_specs=in_specs, out_specs=out_specs, check_vma=False
    )
```

profile of v0, /device:TPU:0, one launch (start us, length us, event | category | flops | bytes accessed | tf_op | source)
XLA Modules:
  0.0 336.2 jit_solution(9609266918678891389)
XLA Ops:
  7.2 0.0 all-gather.4.cloned.1.call-start
  7.2 2.1 bitcast_convert_fusion
  9.3 0.0 all-gather.4.cloned.1.call-update
  9.3 0.0 copy-start.5
  9.3 0.0 copy-start.1
  9.3 0.0 all-reduce.4.cloned.1.call-start
  9.4 40.4 %all-gather.4.cloned.1.call-done = bf16[8192,256]{1,0:T(8,128)(2,1)} async-done(((bf16[1024,256]{1,0:T(8,128)(2,1)}), bf16[8192,256]{1,0:T(8,128)(2,1)}) %all-gather.4.cloned.1.call-update) | async-done | bytes 4194320 | tf_op jit(solution)/shard_map/all_gather | solution.py:16
  49.8 12.4 %fusion.4 = f32[1024,256]{1,0:T(8,128)} fusion(bf16[8192,256]{1,0:T(8,128)(2,1)} %all-gather.4.cloned.1.call-done, bf16[1,8192,1024]{2,1,0:T(8,128)(2,1)} %param.3), kind=kOutput, calls=%fused_computation.4 | convolution fusion | flops 4294967296 | bytes 22020096 | tf_op jit(solution)/shard_map/dot_general | solution.py:14
  62.2 0.0 copy-start
  62.2 0.0 all-reduce.4.cloned.1.call-update
  62.2 0.0 all-gather.6.cloned.1.call-start
  62.3 0.0 copy-done.5
  62.3 52.0 %all-reduce.4.cloned.1.call-done = f32[1024,256]{1,0:T(8,128)} async-done(((f32[1024,256]{1,0:T(8,128)}), f32[1024,256]{1,0:T(8,128)}) %all-reduce.4.cloned.1.call-update) | async-done | bytes 1048592 | tf_op jit(solution)/shard_map/psum | solution.py:23
  114.3 0.0 copy-done.1
  114.3 0.0 copy-start.3
  114.3 3.0 fusion.19
  117.3 0.0 all-gather.6.cloned.1.call-update
  117.3 0.0 all-reduce.6.cloned.1.call-start
  117.3 36.0 %all-gather.6.cloned.1.call-done = bf16[8192,256]{1,0:T(8,128)(2,1)} async-done(((bf16[1024,256]{1,0:T(8,128)(2,1)}), bf16[8192,256]{1,0:T(8,128)(2,1)}) %all-gather.6.cloned.1.call-update) | async-done | bytes 4194320 | tf_op jit(solution)/shard_map/all_gather | solution.py:16
  153.3 0.0 copy-done
  153.3 0.0 copy-done.3
  153.3 14.8 %fusion.15 = f32[1024,256]{1,0:T(8,128)} fusion(bf16[8192,256]{1,0:T(8,128)(2,1)} %all-gather.6.cloned.1.call-done, bf16[1,8192,1024]{2,1,0:T(8,128)(2,1)} %param.3, f32[1024,256]{1,0:T(8,128)S(1)} %copy-done, f32[1024,256]{1,0:T(8,128)S(1)} %copy-done.3, f32[256]{0:T(256)S(1)} %broadcast_multiply_fusion), kind=kOutput, calls=%fused_computation.9 | convolution fusion | flops 4297064448 | bytes 24118272 | tf_op jit(solution)/shard_map/dot_general | solution.py:14
  168.1 0.0 copy-start.2
  168.1 0.0 all-reduce.6.cloned.1.call-update
  168.1 0.2 all-gather.8.cloned.1.call-start
  168.4 51.8 %all-reduce.6.cloned.1.call-done = f32[1024,256]{1,0:T(8,128)} async-done(((f32[1024,256]{1,0:T(8,128)}), f32[1024,256]{1,0:T(8,128)}) %all-reduce.6.cloned.1.call-update) | async-done | bytes 1048592 | tf_op jit(solution)/shard_map/psum | solution.py:23
  220.2 0.0 copy-start.4
  220.2 2.9 fusion.21
  223.1 0.0 all-gather.8.cloned.1.call-update
  223.2 0.0 all-reduce.8.cloned.1.call-start
  223.2 36.0 %all-gather.8.cloned.1.call-done = bf16[8192,256]{1,0:T(8,128)(2,1)} async-done(((bf16[1024,256]{1,0:T(8,128)(2,1)}), bf16[8192,256]{1,0:T(8,128)(2,1)}) %all-gather.8.cloned.1.call-update) | async-done | bytes 4194320 | tf_op jit(solution)/shard_map/all_gather | solution.py:16
  259.2 0.0 copy-done.2
  259.2 0.0 copy-done.4
  259.2 14.8 %fusion.12 = f32[1024,256]{1,0:T(8,128)} fusion(bf16[8192,256]{1,0:T(8,128)(2,1)} %all-gather.8.cloned.1.call-done, bf16[1,8192,1024]{2,1,0:T(8,128)(2,1)} %param.3, f32[1024,256]{1,0:T(8,128)S(1)} %copy-done.2, f32[1024,256]{1,0:T(8,128)S(1)} %copy-done.4, f32[256]{0:T(256)S(1)} %broadcast_multiply_fusion), kind=kOutput, calls=%fused_computation.8 | convolution fusion | flops 4297064448 | bytes 24118272 | tf_op jit(solution)/shard_map/dot_general | solution.py:14
  274.0 0.0 all-reduce.8.cloned.1.call-update
  274.0 52.1 %all-reduce.8.cloned.1.call-done = f32[1024,256]{1,0:T(8,128)} async-done(((f32[1024,256]{1,0:T(8,128)}), f32[1024,256]{1,0:T(8,128)}) %all-reduce.8.cloned.1.call-update) | async-done | bytes 1048592 | tf_op jit(solution)/shard_map/psum | solution.py:23
  326.1 3.3 subtract_bitcast_fusion
  (1 shorter events, 0.0 us)
Async XLA Ops:
  7.2 42.6 %all-gather.4.cloned.1.call-start = ((), (), s32[]{:S(2)}) async-start(), calls=%async_computation | async-start | bytes 4718592 | tf_op jit(solution)/shard_map/all_gather | solution.py:16
  9.3 53.0 %copy-start.5 = (f32[256]{0:T(256)S(1)}, f32[256]{0:T(256)}, u32[]{:S(2)}) copy-start(f32[256]{0:T(256)} %param.5) | copy-start | bytes 3076
  9.3 105.0 %copy-start.1 = (f32[1,1024,256]{2,1,0:T(8,128)S(1)}, f32[1,1024,256]{2,1,0:T(8,128)}, u32[]{:S(2)}) copy-start(f32[1,1024,256]{2,1,0:T(8,128)} %param.4) | copy-start | bytes 3145732
  9.3 105.0 %all-reduce.4.cloned.1.call-start = ((), (), s32[]{:S(2)}) async-start(), calls=%async_computation.1 | async-start | bytes 2097152 | tf_op jit(solution)/shard_map/psum | solution.py:23
  62.2 91.1 %copy-start = (f32[1024,256]{1,0:T(8,128)S(1)}, f32[1024,256]{1,0:T(8,128)}, u32[]{:S(2)}) copy-start(f32[1024,256]{1,0:T(8,128)} %fusion.4) | copy-start | bytes 3145732
  62.2 91.0 %all-gather.6.cloned.1.call-start = ((), (), s32[]{:S(2)}) async-start(), calls=%async_computation.2 | async-start | bytes 4718592 | tf_op jit(solution)/shard_map/all_gather | solution.py:16
  114.3 39.0 %copy-start.3 = (f32[1024,256]{1,0:T(8,128)S(1)}, f32[1024,256]{1,0:T(8,128)}, u32[]{:S(2)}) copy-start(f32[1024,256]{1,0:T(8,128)} %all-reduce.4.cloned.1.call-done) | copy-start | bytes 3145732
  117.3 102.9 %all-reduce.6.cloned.1.call-start = ((), (), s32[]{:S(2)}) async-start(), calls=%async_computation.3 | async-start | bytes 2097152 | tf_op jit(solution)/shard_map/psum | solution.py:23
  168.1 91.1 %copy-start.2 = (f32[1024,256]{1,0:T(8,128)S(1)}, f32[1024,256]{1,0:T(8,128)}, u32[]{:S(2)}) copy-start(f32[1024,256]{1,0:T(8,128)} %fusion.15) | copy-start | bytes 3145732
  168.1 91.0 %all-gather.8.cloned.1.call-start = ((), (), s32[]{:S(2)}) async-start(), calls=%async_computation.4 | async-start | bytes 4718592 | tf_op jit(solution)/shard_map/all_gather | solution.py:16
  220.2 39.0 %copy-start.4 = (f32[1024,256]{1,0:T(8,128)S(1)}, f32[1024,256]{1,0:T(8,128)}, u32[]{:S(2)}) copy-start(f32[1024,256]{1,0:T(8,128)} %all-reduce.6.cloned.1.call-done) | copy-start | bytes 3145732
  223.2 102.9 %all-reduce.8.cloned.1.call-start = ((), (), s32[]{:S(2)}) async-start(), calls=%async_computation.5 | async-start | bytes 2097152 | tf_op jit(solution)/shard_map/psum | solution.py:23
Sparse Core Ops, SparseCore 0:
  10.4 39.2 all-gather.3
  62.4 51.8 all-reduce.3
  117.4 35.8 all-gather.5
  168.2 51.8 all-reduce.5
  223.3 35.8 all-gather.7
  274.1 51.8 all-reduce.7
where the time goes:
time: 336 us
  waiting for transfers between devices  268 us (80%)
  matrix products  42.1 us (13%)
  between operations  14.1 us (4%)
  other arithmetic  11.3 us (3%)
    psum x3, waiting for transfers between devices, agree(): summed = lax.psum(summed_in, 'grp')  156 us
    all_gather x3, waiting for transfers between devices, apply_inverse(): lax.all_gather(shifted, 'col', axis=0, tiled=True)  112 us
    dot_general x3, matrix products, apply_inverse(): lax.dot_general(columns, lax.all_gather(shifted, 'col', axis=0, tiled=Tru...  42.1 us
    convert_element_type x3, other arithmetic, update_paths(): shifted = (right_part + consensus - duals).astype(jnp.bfloat16)  7.97 us
  transfers between devices with their start and end apart: 6, of which 6 were waited for; matrix products, arithmetic and copies ran while one was open for 0% of the time, Pallas kernels for 0%

commit v1 on v0

v1 whole, which is shorter than its diff:
```python
import functools

import jax
import jax.numpy as jnp
from jax import lax
from jax.experimental import pallas as pl
from jax.experimental.pallas import tpu as pltpu
from jax.sharding import PartitionSpec as P

ITERS = 3
FULL_SUMS = 1
LANES = 128
ROUTES = 2
MESH = pl.DeviceIdType.MESH


def gather_plan(bits):
    orders, events = [], []
    for route in range(ROUTES):
        network = list(range(1, bits))
        order = (network if route == 0 else network[::-1]) + [0]
        orders.append(order)
        for place in range(1 << bits):
            mask = sum(1 << order[j] for j in range(bits) if place >> j & 1)
            crossed = place & ((1 << (bits - 1)) - 1)
            other_core = place >> (bits - 1)
            key = 2 * crossed + (3 if crossed else 1) * other_core
            events.append((key, route, mask, place.bit_length()))
    events.sort()
    return orders, [event[1:] for event in events]


def kernel(
    cols, groups, inverse, right_side, penalty, consensus_out, duals_out,
    held, pieces, acc, total_in, duals, right, limit,
    from_low, from_high, to_high, to_low,
    low_rest, high_rest, up_rest, down_rest,
    load_sem, send_sem, recv_sem, up_send, up_recv, down_send, down_recv,
    up_rest_send, up_rest_recv, down_rest_send, down_rest_recv,
):
    rows = right_side.shape[0]
    halves = right_side.shape[1] // LANES
    phases = halves * ITERS
    coarse = phases - low_rest.shape[0]
    width = rows // ROUTES
    chunks, chunk = total_in.shape[1], total_in.shape[3]
    bits = cols.bit_length() - 1
    orders, events = gather_plan(bits)
    last_network = max(i for i, (_, mask, _) in enumerate(events) if not mask & 1)
    me = lax.axis_index("col")
    grp = lax.axis_index("grp")

    def load(source):
        return pltpu.make_async_copy(
            inverse.at[pl.ds(pl.multiple_of(source * rows, rows), rows), :],
            held.at[source],
            load_sem.at[source],
        )

    seen = []
    for _, mask, _ in events:
        if mask not in seen:
            seen.append(mask)
    for mask in seen:
        load(me ^ mask).start()

    barrier = pltpu.get_barrier_semaphore()
    for bit in range(bits):
        pl.semaphore_signal(barrier, inc=1, device_id={"col": me ^ (1 << bit)}, device_id_type=MESH)

    @pl.when(grp > 0)
    def _():
        pl.semaphore_signal(barrier, inc=1, device_id={"grp": grp - 1}, device_id_type=MESH)

    @pl.when(grp < groups - 1)
    def _():
        pl.semaphore_signal(barrier, inc=1, device_id={"grp": grp + 1}, device_id_type=MESH)

    for half in range(halves):
        for j in range(rows // LANES):
            right[half, :, j * LANES:(j + 1) * LANES] = (
                right_side[j * LANES:(j + 1) * LANES, half * LANES:(half + 1) * LANES].T
            )
        limit[half] = jnp.broadcast_to(
            penalty[0:1, half * LANES:(half + 1) * LANES], (LANES, LANES)
        ).T * (1.0 / groups)
        duals[half] = jnp.zeros((LANES, rows), jnp.float32)
        for route in range(ROUTES):
            pieces[half, me, route] = right[half, :, route * width:(route + 1) * width].astype(jnp.bfloat16)

    @pl.when(grp == 0)
    def _():
        from_low[...] = jnp.zeros_like(from_low)
        low_rest[...] = jnp.zeros_like(low_rest)

    @pl.when(grp == groups - 1)
    def _():
        from_high[...] = jnp.zeros_like(from_high)
        high_rest[...] = jnp.zeros_like(high_rest)

    below = jnp.minimum(grp, 1)
    above = jnp.minimum(groups - 1 - grp, 1)
    pl.semaphore_wait(barrier, bits + below + above)

    def hop(t, route, mask, bit):
        block = pieces.at[t, me ^ mask, route]
        return pltpu.make_async_remote_copy(
            src_ref=block,
            dst_ref=block,
            send_sem=send_sem.at[t, route, mask ^ (1 << bit)],
            recv_sem=recv_sem.at[t, route, mask ^ (1 << bit)],
            device_id={"col": me ^ (1 << bit)},
            device_id_type=MESH,
        )

    def arrival(t, route, mask):
        block = pieces.at[t, me ^ mask, route]
        return pltpu.make_async_remote_copy(
            src_ref=block,
            dst_ref=block,
            send_sem=send_sem.at[t, route, mask],
            recv_sem=recv_sem.at[t, route, mask],
            device_id={"col": me ^ 1},
            device_id_type=MESH,
        )

    def start_gather(t):
        stages = list(range(bits))
        for stage in [0] + stages[-1:] + stages[1:-1]:
            for route in range(ROUTES):
                hop(t, route, 0, orders[route][stage]).start()

    def up(t, c):
        return pltpu.make_async_remote_copy(
            src_ref=to_high.at[t, c], dst_ref=from_low.at[t, c],
            send_sem=up_send.at[t, c], recv_sem=up_recv.at[t, c],
            device_id={"grp": lax.rem(grp + 1, groups)}, device_id_type=MESH,
        )

    def down(t, c):
        return pltpu.make_async_remote_copy(
            src_ref=to_low.at[t, c], dst_ref=from_high.at[t, c],
            send_sem=down_send.at[t, c], recv_sem=down_recv.at[t, c],
            device_id={"grp": lax.rem(grp + groups - 1, groups)}, device_id_type=MESH,
        )

    def up_more(t, c):
        return pltpu.make_async_remote_copy(
            src_ref=up_rest.at[t - coarse, c], dst_ref=low_rest.at[t - coarse, c],
            send_sem=up_rest_send.at[t - coarse, c], recv_sem=up_rest_recv.at[t - coarse, c],
            device_id={"grp": lax.rem(grp + 1, groups)}, device_id_type=MESH,
        )

    def down_more(t, c):
        return pltpu.make_async_remote_copy(
            src_ref=down_rest.at[t - coarse, c], dst_ref=high_rest.at[t - coarse, c],
            send_sem=down_rest_send.at[t - coarse, c], recv_sem=down_rest_recv.at[t - coarse, c],
            device_id={"grp": lax.rem(grp + groups - 1, groups)}, device_id_type=MESH,
        )

    going_up = (up, up_more, from_low, low_rest, to_high, up_rest)
    going_down = (down, down_more, from_high, high_rest, to_low, down_rest)

    def send_sum(t, c, value, way):
        head_copy, rest_copy, _, _, head_out, rest_out = way
        head = value.astype(jnp.bfloat16)
        head_out[t, c] = head
        head_copy(t, c).start()

        @pl.when(t >= coarse)
        def _():
            rest_out[t - coarse, c] = (value - head.astype(jnp.float32)).astype(jnp.bfloat16)
            rest_copy(t, c).start()

    def forward_sum(t, c, half, way):
        head_copy, rest_copy, head_in, rest_in, _, _ = way
        head_copy(t, c).wait_recv()

        @pl.when(t >= coarse)
        def _():
            rest_copy(t, c).wait_recv()
            send_sum(t, c, head_in[t, c].astype(jnp.float32) + rest_in[t - coarse, c].astype(jnp.float32) + total_in[half, c], way)

        @pl.when(t < coarse)
        def _():
            send_sum(t, c, head_in[t, c].astype(jnp.float32) + total_in[half, c], way)

    def end_sum(t, c, way):
        head_copy, rest_copy = way[:2]
        head_copy(t, c).wait_recv()

        @pl.when(t >= coarse)
        def _():
            rest_copy(t, c).wait_recv()

    def start_sum(t):
        half = lax.rem(t, halves)

        @pl.when(jnp.logical_and(grp == 0, grp < groups - 1))
        def _():
            for c in range(chunks):
                send_sum(t, c, total_in[half, c], going_up)

        @pl.when(jnp.logical_and(grp == groups - 1, grp > 0))
        def _():
            for c in range(chunks):
                send_sum(t, c, total_in[half, c], going_down)

    lag = min(3, chunks)
    slots = chunks + lag * (groups - 3) if groups > 2 else 0

    def pass_on(t, slot):
        half = lax.rem(t, halves)
        c_up = slot - lag * (grp - 1)
        c_down = slot - lag * (groups - 2 - grp)
        inner = jnp.logical_and(grp > 0, grp < groups - 1)

        @pl.when(jnp.logical_and(inner, jnp.logical_and(c_up >= 0, c_up < chunks)))
        def _():
            forward_sum(t, c_up, half, going_up)

        @pl.when(jnp.logical_and(inner, jnp.logical_and(c_down >= 0, c_down < chunks)))
        def _():
            forward_sum(t, c_down, half, going_down)

    def finish_sum(t):
        @pl.when(jnp.logical_and(grp == groups - 1, grp > 0))
        def _():
            for c in range(chunks):
                end_sum(t, c, going_up)

        @pl.when(jnp.logical_and(grp == 0, grp < groups - 1))
        def _():
            for c in range(chunks):
                end_sum(t, c, going_down)

    def update(t, half):
        @pl.when(t >= coarse)
        def _():
            update_with(t, half, True)

        @pl.when(t < coarse)
        def _():
            update_with(t, half, False)

    def update_with(t, half, with_rest):
        last = t >= phases - halves
        for c in range(chunks):
            for part in range(chunk // LANES):
                inside = slice(part * LANES, (part + 1) * LANES)
                at = c * chunk + part * LANES
                own = total_in[half, c, :, inside]
                summed = (
                    own
                    + from_low[t, c, :, inside].astype(jnp.float32)
                    + from_high[t, c, :, inside].astype(jnp.float32)
                )
                if with_rest:
                    summed = (
                        summed
                        + low_rest[t - coarse, c, :, inside].astype(jnp.float32)
                        + high_rest[t - coarse, c, :, inside].astype(jnp.float32)
                    )
                blended = summed * (1.0 / groups)
                bound = limit[half]
                consensus = blended - jnp.minimum(jnp.maximum(blended, -bound), bound)
                dual = own - consensus
                duals[half, :, at:at + LANES] = dual
                shifted = (right[half, :, at:at + LANES] + consensus - dual).astype(jnp.bfloat16)

                @pl.when(jnp.logical_not(last))
                def _():
                    pieces[t + halves, me, at // width, :, at % width:at % width + LANES] = shifted

                @pl.when(last)
                def _():
                    acc[:, at:at + LANES] = consensus

    def write_out(half):
        for j in range(rows // LANES):
            down_rows = slice(j * LANES, (j + 1) * LANES)
            paths = slice(half * LANES, (half + 1) * LANES)
            consensus_out[down_rows, paths] = acc[:, down_rows].T
            duals_out[down_rows, paths] = duals[half, :, down_rows].T

    start_gather(0)

    def phase(t, carry):
        half = lax.rem(t, halves)
        slot = 0
        for i, (route, mask, stage) in enumerate(events):
            if mask:
                arrival(t, route, mask).wait_recv()
                for later in range(stage, bits):
                    hop(t, route, mask, orders[route][later]).start()
            if i == last_network:
                @pl.when(t < halves - 1)
                def _():
                    start_gather(t + 1)
            if mask not in [event[1] for event in events[:i]]:
                @pl.when(t == 0)
                def _():
                    load(me ^ mask).wait()
            source = me ^ mask
            product = jnp.dot(
                pieces[t, source, route],
                held[source, route * width:(route + 1) * width, :],
                preferred_element_type=jnp.float32,
            )
            if i == 0:
                acc[...] = product
            else:
                acc[...] += product
            due = slots * (i + 1) // max(1, last_network)
            while slot < min(due, slots):
                @pl.when(t > 0)
                def _(slot=slot):
                    pass_on(t - 1, slot)
                slot += 1
        for c in range(chunks):
            at = slice(c * chunk, (c + 1) * chunk)
            total_in[half, c] = acc[:, at] + duals[half, :, at]
        start_sum(t)

        @pl.when(t > 0)
        def _():
            earlier = lax.rem(t - 1, halves)
            finish_sum(t - 1)
            update(t - 1, earlier)

        @pl.when(jnp.logical_and(t >= halves - 1, t < phases - 1))
        def _():
            start_gather(t + 1)

        @pl.when(t == phases - 1)
        def _():
            write_out(halves - 2)

        return carry

    lax.fori_loop(0, phases, phase, 0)
    for slot in range(slots):
        pass_on(phases - 1, slot)
    finish_sum(phases - 1)
    update(phases - 1, halves - 1)
    write_out(halves - 1)

    def drain(t, carry):
        for route in range(ROUTES):
            for mask in range(1, cols):
                arrival(t, route, mask).wait_send()
        for c in range(chunks):
            @pl.when(grp < groups - 1)
            def _():
                up(t, c).wait_send()

                @pl.when(t >= coarse)
                def _():
                    up_more(t, c).wait_send()

            @pl.when(grp > 0)
            def _():
                down(t, c).wait_send()

                @pl.when(t >= coarse)
                def _():
                    down_more(t, c).wait_send()
        return carry

    lax.fori_loop(0, phases, drain, 0)


def on_device(cols, groups, inverse, right_side, penalty):
    rows, paths = right_side.shape[1:]
    halves = paths // LANES
    phases = halves * ITERS
    chunks = rows // LANES if rows >= 4 * LANES else 1
    chunk = rows // chunks
    whole = pl.BlockSpec(memory_space=pltpu.VMEM)
    fine = halves * FULL_SUMS
    sums = pltpu.VMEM((phases, chunks, LANES, chunk), jnp.bfloat16)
    rests = pltpu.VMEM((fine, chunks, LANES, chunk), jnp.bfloat16)
    consensus, duals = pl.pallas_call(
        functools.partial(kernel, cols, groups),
        out_shape=(
            jax.ShapeDtypeStruct((rows, paths), jnp.float32),
            jax.ShapeDtypeStruct((rows, paths), jnp.float32),
        ),
        in_specs=[pl.BlockSpec(memory_space=pl.ANY), whole, whole],
        out_specs=(whole, whole),
        scratch_shapes=[
            pltpu.VMEM((cols, rows, rows), jnp.bfloat16),
            pltpu.VMEM((phases, cols, ROUTES, LANES, rows // ROUTES), jnp.bfloat16),
            pltpu.VMEM((LANES, rows), jnp.float32),
            pltpu.VMEM((halves, chunks, LANES, chunk), jnp.float32),
            pltpu.VMEM((halves, LANES, rows), jnp.float32),
            pltpu.VMEM((halves, LANES, rows), jnp.float32),
            pltpu.VMEM((halves, LANES, LANES), jnp.float32),
            sums, sums, sums, sums,
            rests, rests, rests, rests,
            pltpu.SemaphoreType.DMA((cols,)),
            pltpu.SemaphoreType.DMA((phases, ROUTES, cols)),
            pltpu.SemaphoreType.DMA((phases, ROUTES, cols)),
            pltpu.SemaphoreType.DMA((phases, chunks)),
            pltpu.SemaphoreType.DMA((phases, chunks)),
            pltpu.SemaphoreType.DMA((phases, chunks)),
            pltpu.SemaphoreType.DMA((phases, chunks)),
            pltpu.SemaphoreType.DMA((fine, chunks)),
            pltpu.SemaphoreType.DMA((fine, chunks)),
            pltpu.SemaphoreType.DMA((fine, chunks)),
            pltpu.SemaphoreType.DMA((fine, chunks)),
        ],
        compiler_params=pltpu.CompilerParams(
            collective_id=0, has_side_effects=True, vmem_limit_bytes=60 * 1024 * 1024
        ),
    )(inverse[0], right_side[0], penalty[None, :])
    return consensus, duals[None]


def solution(mesh):
    in_specs = (P("grp", None, "col"), P("grp", "col", None), P())
    out_specs = (P("col", None), P("grp", "col", None))
    return jax.shard_map(
        functools.partial(on_device, mesh.shape["col"], mesh.shape["grp"]),
        mesh=mesh, in_specs=in_specs, out_specs=out_specs, check_vma=False,
    )
```

time: 336 us -> 118 us (0.35)
  waiting for transfers between devices: 268 us -> 0 us
  Pallas kernels: 0 us -> 112 us
  matrix products: 42.1 us -> 0 us
  between operations: 14.1 us -> 0.64 us
  other arithmetic: 11.3 us -> 0 us
  local copies, waits for them, and re-layouts: 0.03 us -> 4.52 us
    psum x3 -> x0, waiting for transfers between devices: 156 us -> none  [agree(): summed = lax.psum(summed_in, 'grp')]
    pallas_call x0 -> x1, Pallas kernels: none -> 112 us  [on_device(): pl.pallas_call(functools.partial(kernel, cols, groups), out_shape=(jax.Sh...]
    all_gather x3 -> x0, waiting for transfers between devices: 112 us -> none  [apply_inverse(): lax.all_gather(shifted, 'col', axis=0, tiled=True)]
    dot_general x3 -> x0, matrix products: 42.1 us -> none  [apply_inverse(): lax.dot_general(columns, lax.all_gather(shifted, 'col', axis=0, tiled=Tru...]
    convert_element_type x3 -> x0, other arithmetic: 7.97 us -> none  [update_paths(): shifted = (right_part + consensus - duals).astype(jnp.bfloat16)]
    unnamed x12 -> x2, local copies, waits for them, and re-layouts: 0.03 us -> 4.52 us
  transfers between devices with their start and end apart: 6 -> 0, of which waited for: 6 -> 0; matrix products, arithmetic and copies ran while one was open for 0% -> 0% of each run, Pallas kernels for 0% -> 0%
where the time goes in v1:
time: 118 us
  Pallas kernels  112 us (95%)
  local copies, waits for them, and re-layouts  4.52 us (4%)
    pallas_call x1, Pallas kernels, on_device(): pl.pallas_call(functools.partial(kernel, cols, groups), out_shape=(jax.Sh...  112 us
    unnamed x2, local copies, waits for them, and re-layouts  4.52 us

profile of v1, /device:TPU:0, one launch (start us, length us, event | category | flops | bytes accessed | tf_op | source)
XLA Modules:
  0.0 117.5 jit_solution(3429117494202507636)
XLA Ops:
  0.6 112.4 %shard_map.50 = (f32[1024,256]{1,0:T(8,128)}, f32[1024,256]{1,0:T(8,128)}) custom-call(bf16[8192,1024]{1,0:T(8,128)(2,1)} %bitcast.4, f32[1024,256]{1,0:T(8,128)} %bitcast.5, f32[1,256]{1,0:T(1,128)} %bitcast.7), custom_call_target="tpu_custom_call" | custom-call | tf_op jit(solution)/shard_map/pallas_call | solution.py:383
  113.0 2.3 %copy.7 = f32[1024,256]{1,0:T(8,128)} copy(f32[1024,256]{1,0:T(8,128)} %get-tuple-element.8) | data formatting | bytes 2097152
  115.3 2.3 %copy.8 = f32[1,1024,256]{2,1,0:T(8,128)} copy(f32[1,1024,256]{2,1,0:T(8,128)} %bitcast.6) | data formatting | bytes 2097152
